TPU v7x, 32 devices: a whole 2x2x4 slice. The times are simulated.
32 devices in a mesh: fsdp: 4 (over z), ctx: 4 (over x, core), tp: 2 (over y).
Axes of the slice: x: 2, y: 2, z: 4, core: 2. Of those that a mesh axis runs over, the one named last changes fastest.
Arguments:
- tokens: bfloat16 [4, 1536, 2048], P('fsdp', 'ctx'), may hold values from -6 to 6
- seq_ids: int32 [4, 1536], P('fsdp'), may hold values from 0 to 2, never falling along the last dimension, each value on 1 to 768 neighbouring positions
- pic_starts: int32 [4, 3], P('fsdp'), may hold values from 0 to 1408, as said below
- pic_lengths: int32 [4, 3], P('fsdp'), may hold values from 128 to 256, as said below
- skip_mask: int32 [4, 1536], P('fsdp', 'ctx'), may hold values 0 or 1
- w_query: bfloat16 [2048, 2048], P('fsdp', 'tp'), may hold values from -0.125 to 0.125
- w_key: bfloat16 [2048, 512], P('fsdp', 'tp'), may hold values from -0.125 to 0.125
- w_value: bfloat16 [2048, 512], P('fsdp', 'tp'), may hold values from -0.125 to 0.125
- w_out: bfloat16 [2048, 2048], P('tp', 'fsdp'), may hold values from -1 to 1
- w_gate: bfloat16 [2048, 5632], P('fsdp', 'tp'), may hold values from -0.125 to 0.125
- w_up: bfloat16 [2048, 5632], P('fsdp', 'tp'), may hold values from -0.125 to 0.125
- w_down: bfloat16 [5632, 2048], P('tp', 'fsdp'), may hold values from -0.078125 to 0.078125
- gain_attn: bfloat16 [2048], P('fsdp'), may hold values from 0.25 to 1.75
- gain_ffn: bfloat16 [2048], P('fsdp'), may hold values from 0.25 to 1.75
- cotangent: bfloat16 [4, 1536, 2048], P('fsdp', 'ctx'), may hold values from -6 to 6
Outputs:
- output: bfloat16 [4, 1536, 2048], P('fsdp', 'ctx')
- input_grad: bfloat16 [4, 1536, 2048], P('fsdp', 'ctx')
- grad_query: float32 [2048, 2048], P('fsdp', 'tp')
- grad_key: float32 [2048, 512], P('fsdp', 'tp')
- grad_value: float32 [2048, 512], P('fsdp', 'tp')
- grad_out: float32 [2048, 2048], P('tp', 'fsdp')
- grad_gate: float32 [2048, 5632], P('fsdp', 'tp')
- grad_up: float32 [2048, 5632], P('fsdp', 'tp')
- grad_down: float32 [5632, 2048], P('tp', 'fsdp')
- grad_gain_attn: float32 [2048], P('fsdp')
- grad_gain_ffn: float32 [2048], P('fsdp')
Inputs may be any that keep to these rules, and one draw needn't show every extreme that they name: `pic_starts`: picture p of a row (counting from 0) lies inside positions p * 2 * 256 to (p + 1) * 2 * 256 - 1, so pictures never intersect; it may start anywhere in that range where it fits. `pic_lengths`: every row has a picture of exactly 256 positions and another of exactly 128.
All inputs are finite; a program needn't handle non-finite values. No bound on the sum of `skip_mask` on one device may be relied on, other than what follows from the above.
Results may differ from a plain program's by a relative error of at most 0.022.
Values may be sent and summed in bfloat16 or wider, within the bound.
No kernel may reach another device: no remote copies, remote signals or barrier semaphores. Data moves between devices by JAX's collectives and lax.ppermute only.
A program may use at most 256 MiB of HBM per device.

v0:
```python
import math
import jax
import jax.numpy as jnp
from jax import lax
from jax.sharding import PartitionSpec as P

HEAD = 128
norm_eps = 1e-05
rope_base = 10000.0


def rotate(values_in, positions, sign):
    half_width = values_in.shape[-1] // 2
    frequency = jnp.power(
        rope_base, -jnp.arange(half_width, dtype=jnp.float32) * 2.0 / values_in.shape[-1]
    )
    angles = positions.astype(jnp.float32)[:, None] * frequency[None, :]
    cosine = jnp.cos(angles)[:, None, :]
    sine_val = sign * jnp.sin(angles)[:, None, :]
    first_half = values_in[..., :half_width]
    second = values_in[..., half_width:]
    return jnp.concatenate(
        [first_half * cosine - second * sine_val, second * cosine + first_half * sine_val], axis=-1
    )


def picture_ids(starts, lengths, positions):
    inside = (positions[:, None] >= starts[None, :]) & (
        positions[:, None] < starts[None, :] + lengths[None, :]
    )
    numbers = jnp.arange(1, starts.shape[0] + 1, dtype=jnp.int32)
    return jnp.sum(jnp.where(inside, numbers[None, :], 0), axis=1)


def allowed_mask(query_pos, key_pos, query_doc, key_doc, query_pic, key_pic):
    same_doc = query_doc[:, None] == key_doc[None, :]
    causal = key_pos[None, :] <= query_pos[:, None]
    picture = (query_pic[:, None] == key_pic[None, :]) & (query_pic[:, None] > 0)
    return same_doc & (causal | picture)


def norm_back(d_normed, hat, inv_rms, gain):
    scaled = d_normed * gain
    return inv_rms * (scaled - hat * jnp.mean(scaled * hat, axis=-1, keepdims=True))


def body(
    tokens,
    seq_ids,
    pic_starts,
    pic_lengths,
    skip_mask,
    w_query,
    w_key,
    w_value,
    w_out,
    w_gate,
    w_up,
    w_down,
    gain_attn,
    gain_ffn,
    cotangent,
):
    tok_rows = tokens.shape[1]
    seq_len = seq_ids.shape[1]
    local_q = w_query.shape[1] // HEAD
    local_kv = w_key.shape[1] // HEAD
    group_size = local_q // local_kv
    query_scale = 1.0 / math.sqrt(HEAD)
    offset = lax.axis_index("ctx") * tok_rows
    positions = offset + jnp.arange(tok_rows, dtype=jnp.int32)
    all_pos = jnp.arange(seq_len, dtype=jnp.int32)
    pic_all = picture_ids(pic_starts[0], pic_lengths[0], all_pos)
    doc_all = seq_ids[0]
    query_doc = lax.dynamic_slice_in_dim(doc_all, offset, tok_rows)
    query_pic = lax.dynamic_slice_in_dim(pic_all, offset, tok_rows)
    allowed = allowed_mask(positions, all_pos, query_doc, doc_all, query_pic, pic_all)

    def attn_weights():
        return (
            lax.all_gather(w_query, "fsdp", axis=0, tiled=True),
            lax.all_gather(w_key, "fsdp", axis=0, tiled=True),
            lax.all_gather(w_value, "fsdp", axis=0, tiled=True),
            lax.all_gather(w_out, "fsdp", axis=1, tiled=True),
            lax.all_gather(gain_attn, "fsdp", axis=0, tiled=True),
        )

    def ffn_weights():
        return (
            lax.all_gather(w_gate, "fsdp", axis=0, tiled=True),
            lax.all_gather(w_up, "fsdp", axis=0, tiled=True),
            lax.all_gather(w_down, "fsdp", axis=1, tiled=True),
            lax.all_gather(gain_ffn, "fsdp", axis=0, tiled=True),
        )

    inputs_f = tokens[0].astype(jnp.float32)
    full_query, full_key, full_value, full_out, gain_one = attn_weights()
    inv_one = lax.rsqrt(jnp.mean(inputs_f * inputs_f, axis=-1, keepdims=True) + norm_eps)
    hat_one = inputs_f * inv_one
    normed_one = (hat_one * gain_one.astype(jnp.float32)).astype(jnp.bfloat16)
    query_pre = jnp.dot(normed_one, full_query, preferred_element_type=jnp.float32)
    key_pre = jnp.dot(normed_one, full_key, preferred_element_type=jnp.float32)
    value_pre = jnp.dot(normed_one, full_value, preferred_element_type=jnp.float32)
    queries = (
        rotate(query_pre.reshape(tok_rows, local_q, HEAD), positions, 1.0) * query_scale
    ).astype(jnp.bfloat16)
    keys_local = rotate(key_pre.reshape(tok_rows, local_kv, HEAD), positions, 1.0).astype(
        jnp.bfloat16
    )
    values_local = value_pre.astype(jnp.bfloat16)
    keys_all, values_all = (
        lax.all_gather(keys_local.reshape(tok_rows, local_kv * HEAD), "ctx", axis=0, tiled=True),
        lax.all_gather(values_local, "ctx", axis=0, tiled=True),
    )
    query_groups = queries.reshape(tok_rows, local_kv, group_size, HEAD)
    key_heads = keys_all.reshape(seq_len, local_kv, HEAD)
    value_heads = values_all.reshape(seq_len, local_kv, HEAD)
    head_outs = []
    log_totals = []
    for kv_index in range(local_kv):
        scores = jnp.einsum(
            "qgd,kd->gqk",
            query_groups[:, kv_index],
            key_heads[:, kv_index],
            preferred_element_type=jnp.float32,
        )
        masked = jnp.where(allowed[None], scores, -1e30)
        row_max = jnp.max(masked, axis=-1, keepdims=True)
        exp_scores = jnp.exp(masked - row_max)
        row_total = jnp.sum(exp_scores, axis=-1, keepdims=True)
        soft_b = (exp_scores / row_total).astype(jnp.bfloat16)
        head_outs.append(
            jnp.einsum(
                "gqk,kd->qgd", soft_b, value_heads[:, kv_index], preferred_element_type=jnp.float32
            )
        )
        log_totals.append(row_max + jnp.log(row_total))
    head_out = jnp.stack(head_outs, axis=1).reshape(tok_rows, local_q * HEAD).astype(jnp.bfloat16)
    attn = lax.psum(jnp.dot(head_out, full_out, preferred_element_type=jnp.float32), "tp")
    keep_f = skip_mask[0].astype(jnp.float32)[:, None]
    mid = inputs_f + keep_f * attn
    full_gate, full_up, full_down, gain_two = ffn_weights()
    inv_two = lax.rsqrt(jnp.mean(mid * mid, axis=-1, keepdims=True) + norm_eps)
    hat_two = mid * inv_two
    normed_two = (hat_two * gain_two.astype(jnp.float32)).astype(jnp.bfloat16)
    gate_act = jnp.dot(normed_two, full_gate, preferred_element_type=jnp.float32)
    up_act = jnp.dot(normed_two, full_up, preferred_element_type=jnp.float32)
    hidden_b = (jax.nn.silu(gate_act) * up_act).astype(jnp.bfloat16)
    ffn = lax.psum(
        jnp.dot(hidden_b, full_down, preferred_element_type=jnp.float32).astype(jnp.bfloat16), "tp"
    ).astype(jnp.float32)
    output = (mid + keep_f * ffn).astype(jnp.bfloat16)
    full_gate, full_up, full_down, gain_two = ffn_weights()
    d_out_f = cotangent[0].astype(jnp.float32)
    d_ffn = (keep_f * d_out_f).astype(jnp.bfloat16)
    grad_down = jnp.einsum("tf,td->fd", hidden_b, d_ffn, preferred_element_type=jnp.float32)
    d_hidden = jnp.einsum("td,fd->tf", d_ffn, full_down, preferred_element_type=jnp.float32)
    sigmoid_gate = jax.nn.sigmoid(gate_act)
    d_up = (d_hidden * (gate_act * sigmoid_gate)).astype(jnp.bfloat16)
    d_gate = (d_hidden * up_act * sigmoid_gate * (1.0 + gate_act * (1.0 - sigmoid_gate))).astype(
        jnp.bfloat16
    )
    grad_gate = jnp.einsum("td,tf->df", normed_two, d_gate, preferred_element_type=jnp.float32)
    grad_up = jnp.einsum("td,tf->df", normed_two, d_up, preferred_element_type=jnp.float32)
    d_norm_part = jnp.einsum(
        "tf,df->td", d_gate, full_gate, preferred_element_type=jnp.float32
    ) + jnp.einsum("tf,df->td", d_up, full_up, preferred_element_type=jnp.float32)
    d_norm_two = lax.psum(d_norm_part, "tp")
    grad_gain_two = jnp.sum(d_norm_two * hat_two, axis=0)
    d_mid = d_out_f + norm_back(d_norm_two, hat_two, inv_two, gain_two.astype(jnp.float32))
    full_query, full_key, full_value, full_out, gain_one = attn_weights()
    d_attn = (keep_f * d_mid).astype(jnp.bfloat16)
    grad_out = jnp.einsum("tc,td->cd", head_out, d_attn, preferred_element_type=jnp.float32)
    d_head = jnp.einsum("td,cd->tc", d_attn, full_out, preferred_element_type=jnp.float32).astype(
        jnp.bfloat16
    )
    d_head_groups = d_head.reshape(tok_rows, local_kv, group_size, HEAD)
    d_query_list = []
    d_key_list = []
    d_value_list = []
    for kv_index in range(local_kv):
        scores = jnp.einsum(
            "qgd,kd->gqk",
            query_groups[:, kv_index],
            key_heads[:, kv_index],
            preferred_element_type=jnp.float32,
        )
        soft_f = jnp.where(allowed[None], jnp.exp(scores - log_totals[kv_index]), 0.0)
        soft_b = soft_f.astype(jnp.bfloat16)
        d_soft = jnp.einsum(
            "qgd,kd->gqk",
            d_head_groups[:, kv_index],
            value_heads[:, kv_index],
            preferred_element_type=jnp.float32,
        )
        row_delta = jnp.sum(soft_f * d_soft, axis=-1, keepdims=True)
        d_scores = (soft_f * (d_soft - row_delta)).astype(jnp.bfloat16)
        d_query_list.append(
            jnp.einsum(
                "gqk,kd->qgd", d_scores, key_heads[:, kv_index], preferred_element_type=jnp.float32
            )
        )
        d_key_list.append(
            jnp.einsum(
                "gqk,qgd->kd",
                d_scores,
                query_groups[:, kv_index],
                preferred_element_type=jnp.float32,
            )
        )
        d_value_list.append(
            jnp.einsum(
                "gqk,qgd->kd",
                soft_b,
                d_head_groups[:, kv_index],
                preferred_element_type=jnp.float32,
            )
        )
    d_keys_all = jnp.stack(d_key_list, axis=1).reshape(seq_len, local_kv * HEAD)
    d_values_all = jnp.stack(d_value_list, axis=1).reshape(seq_len, local_kv * HEAD)
    d_keys, d_values = (
        lax.psum_scatter(
            d_keys_all.astype(jnp.bfloat16), "ctx", scatter_dimension=0, tiled=True
        ).astype(jnp.float32),
        lax.psum_scatter(
            d_values_all.astype(jnp.bfloat16), "ctx", scatter_dimension=0, tiled=True
        ).astype(jnp.float32),
    )
    d_queries = jnp.stack(d_query_list, axis=1).reshape(tok_rows, local_q, HEAD)
    d_query_pre = (
        (rotate(d_queries, positions, -1.0) * query_scale)
        .reshape(tok_rows, local_q * HEAD)
        .astype(jnp.bfloat16)
    )
    d_key_pre = (
        rotate(d_keys.reshape(tok_rows, local_kv, HEAD), positions, -1.0)
        .reshape(tok_rows, local_kv * HEAD)
        .astype(jnp.bfloat16)
    )
    d_value_pre = d_values.astype(jnp.bfloat16)
    grad_query = jnp.einsum(
        "td,tc->dc", normed_one, d_query_pre, preferred_element_type=jnp.float32
    )
    grad_key = jnp.einsum("td,tc->dc", normed_one, d_key_pre, preferred_element_type=jnp.float32)
    grad_value = jnp.einsum(
        "td,tc->dc", normed_one, d_value_pre, preferred_element_type=jnp.float32
    )
    d_norm_part_one = (
        jnp.einsum("tc,dc->td", d_query_pre, full_query, preferred_element_type=jnp.float32)
        + jnp.einsum("tc,dc->td", d_key_pre, full_key, preferred_element_type=jnp.float32)
        + jnp.einsum("tc,dc->td", d_value_pre, full_value, preferred_element_type=jnp.float32)
    )
    d_norm_one = lax.psum(d_norm_part_one.astype(jnp.bfloat16), "tp").astype(jnp.float32)
    grad_gain_one = jnp.sum(d_norm_one * hat_one, axis=0)
    input_grad = (
        d_mid + norm_back(d_norm_one, hat_one, inv_one, gain_one.astype(jnp.float32))
    ).astype(jnp.bfloat16)
    (
        shard_query,
        shard_key,
        shard_value,
        shard_out,
        shard_gain_one,
        shard_gate,
        shard_up,
        shard_down,
        shard_gain_two,
    ) = (
        lax.psum_scatter(
            grad_query.astype(jnp.bfloat16), "fsdp", scatter_dimension=0, tiled=True
        ).astype(jnp.float32),
        lax.psum_scatter(
            grad_key.astype(jnp.bfloat16), "fsdp", scatter_dimension=0, tiled=True
        ).astype(jnp.float32),
        lax.psum_scatter(
            grad_value.astype(jnp.bfloat16), "fsdp", scatter_dimension=0, tiled=True
        ).astype(jnp.float32),
        lax.psum_scatter(
            grad_out.astype(jnp.bfloat16), "fsdp", scatter_dimension=1, tiled=True
        ).astype(jnp.float32),
        lax.psum_scatter(
            grad_gain_one.astype(jnp.bfloat16), "fsdp", scatter_dimension=0, tiled=True
        ).astype(jnp.float32),
        lax.psum_scatter(
            grad_gate.astype(jnp.bfloat16), "fsdp", scatter_dimension=0, tiled=True
        ).astype(jnp.float32),
        lax.psum_scatter(
            grad_up.astype(jnp.bfloat16), "fsdp", scatter_dimension=0, tiled=True
        ).astype(jnp.float32),
        lax.psum_scatter(
            grad_down.astype(jnp.bfloat16), "fsdp", scatter_dimension=1, tiled=True
        ).astype(jnp.float32),
        lax.psum_scatter(
            grad_gain_two.astype(jnp.bfloat16), "fsdp", scatter_dimension=0, tiled=True
        ).astype(jnp.float32),
    )
    summed = (
        lax.psum(shard_query.astype(jnp.bfloat16), "ctx").astype(jnp.float32),
        lax.psum(shard_key.astype(jnp.bfloat16), "ctx").astype(jnp.float32),
        lax.psum(shard_value.astype(jnp.bfloat16), "ctx").astype(jnp.float32),
        lax.psum(shard_out.astype(jnp.bfloat16), "ctx").astype(jnp.float32),
        lax.psum(shard_gate.astype(jnp.bfloat16), "ctx").astype(jnp.float32),
        lax.psum(shard_up.astype(jnp.bfloat16), "ctx").astype(jnp.float32),
        lax.psum(shard_down.astype(jnp.bfloat16), "ctx").astype(jnp.float32),
        lax.psum(shard_gain_one.astype(jnp.bfloat16), "ctx").astype(jnp.float32),
        lax.psum(shard_gain_two.astype(jnp.bfloat16), "ctx").astype(jnp.float32),
    )
    return (
        output[None],
        input_grad[None],
        summed[0],
        summed[1],
        summed[2],
        summed[3],
        summed[4],
        summed[5],
        summed[6],
        summed[7],
        summed[8],
    )


def solution(mesh):
    placed = (
        P("fsdp", "ctx", None),
        P("fsdp", None),
        P("fsdp", None),
        P("fsdp", None),
        P("fsdp", "ctx"),
        P("fsdp", "tp"),
        P("fsdp", "tp"),
        P("fsdp", "tp"),
        P("tp", "fsdp"),
        P("fsdp", "tp"),
        P("fsdp", "tp"),
        P("tp", "fsdp"),
        P("fsdp"),
        P("fsdp"),
        P("fsdp", "ctx", None),
    )
    return jax.shard_map(
        body,
        mesh=mesh,
        in_specs=placed,
        out_specs=(
            P("fsdp", "ctx", None),
            P("fsdp", "ctx", None),
            P("fsdp", "tp"),
            P("fsdp", "tp"),
            P("fsdp", "tp"),
            P("tp", "fsdp"),
            P("fsdp", "tp"),
            P("fsdp", "tp"),
            P("tp", "fsdp"),
            P("fsdp"),
            P("fsdp"),
        ),
        check_vma=False,
    )
```

profile of v0, /device:TPU:0, one launch (start us, length us, event | category | flops | bytes accessed | tf_op | source)
XLA Modules:
  0.0 2267.5 jit_solution(3418881602823138451)
XLA Ops:
  12.6 13.7 all-gather
  28.8 11.5 all-gather.10.cloned.1.call-done
  42.2 8.6 all_gather.44
  51.9 17.4 all-gather.12.cloned.1.call-done
  69.3 2.3 copy.103
  71.6 2.0 fusion.73
  73.7 9.0 all_gather.46
  82.7 68.4 %all-gather.14.cloned.1.call-done = bf16[2048,1024]{1,0:T(8,128)(2,1)} async-done(((bf16[512,1024]{1,0:T(8,128)(2,1)}), bf16[2048,1024]{1,0:T(8,128)(2,1)}) %all-gather.14.cloned.1.call-update) | async-done | bytes 4194320 | tf_op jit(solution)/shard_map/all_gather | solution.py:81
  151.2 6.6 copy.105
  157.8 5.0 fusion.71
  166.3 2.4 fusion.69
  170.3 3.3 fusion.12
  175.4 2.7 fusion.79
  178.2 2.9 fusion.80
  181.2 50.7 %all-gather.16.cloned.1.call-done = bf16[1024,2048]{1,0:T(8,128)(2,1)} async-done(((bf16[1024,512]{1,0:T(8,128)(2,1)}), bf16[1024,2048]{1,0:T(8,128)(2,1)}) %all-gather.16.cloned.1.call-update) | async-done | bytes 4194320 | tf_op jit(solution)/shard_map/all_gather | solution.py:84
  231.9 5.7 fusion.102
  239.8 11.9 all-gather.1
  251.8 70.4 %all-reduce.11.cloned.1.call-done = f32[384,2048]{1,0:T(8,128)} async-done(((f32[384,2048]{1,0:T(8,128)}), f32[384,2048]{1,0:T(8,128)}) %all-reduce.11.cloned.1.call-update) | async-done | bytes 3145744 | tf_op jit(solution)/shard_map/psum | solution.py:139
  322.1 3.0 multiply_reduce_fusion.2
  326.6 198.1 %all-gather.20.cloned.1.call-done = bf16[2048,2816]{1,0:T(8,128)(2,1)} async-done(((bf16[512,2816]{1,0:T(8,128)(2,1)}), bf16[2048,2816]{1,0:T(8,128)(2,1)}) %all-gather.20.cloned.1.call-update) | async-done | bytes 11534352 | tf_op jit(solution)/shard_map/all_gather | solution.py:91
  524.7 11.4 fusion.104
  536.2 189.5 %all-gather.18.cloned.1.call-done = bf16[2048,2816]{1,0:T(8,128)(2,1)} async-done(((bf16[512,2816]{1,0:T(8,128)(2,1)}), bf16[2048,2816]{1,0:T(8,128)(2,1)}) %all-gather.18.cloned.1.call-update) | async-done | bytes 11534352 | tf_op jit(solution)/shard_map/all_gather | solution.py:90
  725.6 11.4 fusion.103
  737.1 189.5 %all-gather.22.cloned.1.call-done = bf16[2816,2048]{1,0:T(8,128)(2,1)} async-done(((bf16[2816,512]{1,0:T(8,128)(2,1)}), bf16[2816,2048]{1,0:T(8,128)(2,1)}) %all-gather.22.cloned.1.call-update) | async-done | bytes 11534352 | tf_op jit(solution)/shard_map/all_gather | solution.py:92
  926.6 12.9 multiply_convert_fusion
  939.5 9.1 fusion.105
  948.6 10.6 convolution_add_fusion
  959.3 84.0 %all-reduce.13.cloned.1.call-done = f32[384,2048]{1,0:T(8,128)} async-done(((f32[384,2048]{1,0:T(8,128)}), f32[384,2048]{1,0:T(8,128)}) %all-reduce.13.cloned.1.call-update) | async-done | bytes 3145744 | tf_op jit(solution)/shard_map/psum | solution.py:168
  1043.4 3.4 multiply_reduce_fusion
  1049.8 2.7 convolution_convert_fusion.8
  1052.5 2.8 reshape.370
  1056.7 6.1 fusion.87
  1062.8 5.7 fusion.62
  1071.6 2.3 copy.150
  1074.0 16.4 fusion.3
  1090.4 13.9 fusion.5
  1110.8 2.3 copy.148
  1113.2 3.3 convolution_convert_fusion.6
  1116.6 20.1 reduce-scatter.28.cloned.1.call-done
  1137.9 3.3 convolution_convert_fusion.7
  1141.2 6.6 convolution_convert_fusion.3
  1148.3 3.3 convolution_bitcast_fusion.3
  1151.6 3.2 convolution_bitcast_fusion.2
  1156.5 4.5 convolution_convert_fusion.4
  1161.1 11.0 convolution_convert_fusion.2
  1172.2 10.7 convolution_convert_fusion
  1183.2 10.8 convolution_convert_fusion.1
  1194.0 10.9 convolution_convert_fusion.5
  1210.1 63.4 %reduce-scatter.20.cloned.1.call-done = bf16[1024,512]{1,0:T(8,128)(2,1)} async-done(((bf16[1024,2048]{1,0:T(8,128)(2,1)}), bf16[1024,512]{1,0:T(8,128)(2,1)}) %reduce-scatter.20.cloned.1.call-update) | async-done | bytes 1048592 | tf_op jit(solution)/shard_map/reduce_scatter | solution.py:278
  1273.5 80.1 %reduce-scatter.14.cloned.1.call-done = bf16[512,1024]{1,0:T(8,128)(2,1)} async-done(((bf16[2048,1024]{1,0:T(8,128)(2,1)}), bf16[512,1024]{1,0:T(8,128)(2,1)}) %reduce-scatter.14.cloned.1.call-update) | async-done | bytes 1048592 | tf_op jit(solution)/shard_map/reduce_scatter | solution.py:269
  1353.6 197.7 %reduce-scatter.26.cloned.1.call-done = bf16[2816,512]{1,0:T(8,128)(2,1)} async-done(((bf16[2816,2048]{1,0:T(8,128)(2,1)}), bf16[2816,512]{1,0:T(8,128)(2,1)}) %reduce-scatter.26.cloned.1.call-update) | async-done | bytes 2883600 | tf_op jit(solution)/shard_map/reduce_scatter | solution.py:290
  1551.3 198.2 %reduce-scatter.24.cloned.1.call-done = bf16[512,2816]{1,0:T(8,128)(2,1)} async-done(((bf16[2048,2816]{1,0:T(8,128)(2,1)}), bf16[512,2816]{1,0:T(8,128)(2,1)}) %reduce-scatter.24.cloned.1.call-update) | async-done | bytes 2883600 | tf_op jit(solution)/shard_map/reduce_scatter | solution.py:287
  1749.5 198.2 %reduce-scatter.22.cloned.1.call-done = bf16[512,2816]{1,0:T(8,128)(2,1)} async-done(((bf16[2048,2816]{1,0:T(8,128)(2,1)}), bf16[512,2816]{1,0:T(8,128)(2,1)}) %reduce-scatter.22.cloned.1.call-update) | async-done | bytes 2883600 | tf_op jit(solution)/shard_map/reduce_scatter | solution.py:284
  1949.6 88.1 %all-reduce.17.cloned.1.call-done = (bf16[384,2048]{1,0:T(8,128)(2,1)}, bf16[384,2048]{1,0:T(8,128)(2,1)}) async-done(((bf16[384,2048]{1,0:T(8,128)(2,1)}, bf16[384,2048]{1,0:T(8,128)(2,1)}), (bf16[384,2048]{1,0:T(8,128)(2,1)}, bf16[384,2048]{1,0:T(8,128)(2,1)})) %all-reduce.17.cloned.1.call-update) | async-done | bytes 3145744 | tf_op jit(solution)/shard_map/psum | solution.py:149
  2037.7 3.0 fusion.38
  2040.7 11.9 all-reduce.4
  2052.7 6.4 all-reduce.2
  2060.2 3.1 fusion.67
  2064.2 2.2 fusion.68
  2066.4 176.6 %all-reduce.15.cloned.1.call-done = (bf16[512,1024]{1,0:T(8,128)(2,1)}, bf16[512,256]{1,0:T(8,128)(2,1)}, bf16[512,256]{1,0:T(8,128)(2,1)}, bf16[1024,512]{1,0:T...) async-done(((bf16[512,1024]{1,0:T(8,128)(2,1)}, bf16[512,256]{1,0:T(8,128)(2,1)}, bf16[512,256]{1,0:T(8,128)(2,1)}, ...) | async-done | bytes 11272208 | tf_op jit(solution)/shard_map/psum | solution.py:298
  2246.6 2.9 convert_element_type.282
  2251.1 2.9 convert_element_type.290
  2254.1 2.9 convert_element_type.292
  2257.0 3.4 convert_element_type.294
  (206 shorter events, 52.9 us)
Async XLA Ops:
  7.2 5.0 copy-start.4
  7.2 19.1 copy-start.44
  7.2 19.1 copy-start.45
  7.2 33.1 %all-gather.10.cloned.1.call-start = ((), (), s32[]{:S(2)}) async-start(), calls=%async_computation.9 | async-start | bytes 1310720 | tf_op jit(solution)/shard_map/all_gather | solution.py:83
  7.9 61.4 %all-gather.12.cloned.1.call-start = ((), (), s32[]{:S(2)}) async-start(), calls=%async_computation.10 | async-start | bytes 1310720 | tf_op jit(solution)/shard_map/all_gather | solution.py:82
  8.7 142.5 %all-gather.14.cloned.1.call-start = ((), (), s32[]{:S(2)}) async-start(), calls=%async_computation.11 | async-start | bytes 5242880 | tf_op jit(solution)/shard_map/all_gather | solution.py:81
  9.4 222.5 %all-gather.16.cloned.1.call-start = ((), (), s32[]{:S(2)}) async-start(), calls=%async_computation.12 | async-start | bytes 5242880 | tf_op jit(solution)/shard_map/all_gather | solution.py:84
  10.0 312.1 %all-reduce.11.cloned.1.call-start = ((), (), s32[]{:S(2)}) async-start(), calls=%async_computation.13 | async-start | bytes 6291456 | tf_op jit(solution)/shard_map/psum | solution.py:139
  12.6 145.2 %copy-start.39 = (f32[384]{0:T(512)}, f32[384]{0:T(512)S(1)}, u32[]{:S(2)}) copy-start(f32[384]{0:T(512)S(1)} %add_rsqrt_fusion.1) | copy-start | bytes 4612
  26.3 131.5 %copy-start.35 = (f32[4,1,512]{2,1,0:T(1,128)}, f32[4,1,512]{2,1,0:T(1,128)S(1)}, u32[]{:S(2)}) copy-start(f32[4,1,512]{2,1,0:T(1,128)S(1)} %convert_element_type.301) | copy-start | bytes 24580
  27.6 135.2 %copy-start.26 = (f32[384,64]{0,1:T(8,128)}, f32[384,64]{0,1:T(8,128)S(1)}, u32[]{:S(2)}) copy-start(f32[384,64]{0,1:T(8,128)S(1)} %get-tuple-element.53) | copy-start | bytes 294916
  28.8 149.4 %copy-start.7 = (pred[384,1536]{0,1:T(8,128)(4,1)}, pred[384,1536]{0,1:T(8,128)(4,1)S(1)}, u32[]{:S(2)}) copy-start(pred[384,1536]{0,1:T(8,128)(4,1)S(1)} %fusion.58) | copy-start | bytes 1769476
  164.7 4.0 copy-start.16
  170.3 5.1 copy-start
  173.6 4.5 copy-start.1
  173.6 1.8 copy-start.22
  181.2 56.4 %copy-start.19 = (bf16[384,2,4,128]{0,3,2,1:T(8,128)(2,1)}, bf16[384,2,4,128]{0,3,2,1:T(8,128)(2,1)S(1)}, u32[]{:S(2)}) copy-start(bf16[384,2,4,128]{0,3,2,1:T(8,128)(2,1)S(1)} %pad_maximum_fusion.1) | copy-start | bytes 2359300
  237.7 287.1 %all-gather.20.cloned.1.call-start = ((), (), s32[]{:S(2)}) async-start(), calls=%async_computation.15 | async-start | bytes 14417920 | tf_op jit(solution)/shard_map/all_gather | solution.py:91
  238.2 13.5 copy-start.42
  238.3 487.4 %all-gather.18.cloned.1.call-start = ((), (), s32[]{:S(2)}) async-start(), calls=%async_computation.14 | async-start | bytes 14417920 | tf_op jit(solution)/shard_map/all_gather | solution.py:90
  239.0 687.6 %all-gather.22.cloned.1.call-start = ((), (), s32[]{:S(2)}) async-start(), calls=%async_computation.16 | async-start | bytes 14417920 | tf_op jit(solution)/shard_map/all_gather | solution.py:92
  239.8 803.6 %all-reduce.13.cloned.1.call-start = ((), (), s32[]{:S(2)}) async-start(), calls=%async_computation.17 | async-start | bytes 6291456 | tf_op jit(solution)/shard_map/psum | solution.py:168
  251.7 796.0 %copy-start.37 = (f32[384]{0:T(512)}, f32[384]{0:T(512)S(1)}, u32[]{:S(2)}) copy-start(f32[384]{0:T(512)S(1)} %convert_reduce_fusion) | copy-start | bytes 4612
  939.5 9.1 copy-start.47
  939.5 9.1 copy-start.48
  959.3 153.9 %reduce-scatter.30.cloned.1.call-start = ((), (), s32[]{:S(2)}) async-start(), calls=%async_computation.26 | async-start | bytes 983040
  1043.4 3.4 copy-start.12
  1043.4 3.4 copy-start.28
  1046.8 3.0 copy-start.13
  1056.7 6.1 copy-start.8
  1056.7 11.9 slice-start
  1056.7 11.9 slice-start.1
  1062.8 5.8 slice-start.2
  1073.9 62.7 %reduce-scatter.28.cloned.1.call-start = ((), (), s32[]{:S(2)}) async-start(), calls=%async_computation.25 | async-start | bytes 983040
  1073.9 16.4 copy-start.9
  1090.4 14.0 copy-start.15
  1104.4 2.2 copy-start.3
  1104.4 3.7 copy-start.2
  1109.8 3.4 copy-start.36
  1109.8 3.4 copy-start.40
  1113.1 24.7 %copy-start.27 = (f32[384,64]{0,1:T(8,128)S(1)}, f32[384,64]{0,1:T(8,128)}, u32[]{:S(2)}) copy-start(f32[384,64]{0,1:T(8,128)} %copy-done.26) | copy-start | bytes 294916
  1113.1 24.7 %copy-start.31 = (f32[384,64]{0,1:T(8,128)S(1)}, f32[384,64]{0,1:T(8,128)}, u32[]{:S(2)}) copy-start(f32[384,64]{0,1:T(8,128)} %get-tuple-element.51) | copy-start | bytes 294916
  1113.1 96.9 %reduce-scatter.18.cloned.1.call-start = ((), (), s32[]{:S(2)}) async-start(), calls=%async_computation.20 | async-start | bytes 1310720 | tf_op jit(solution)/shard_map/reduce_scatter | solution.py:275
  1116.5 93.6 %reduce-scatter.16.cloned.1.call-start = ((), (), s32[]{:S(2)}) async-start(), calls=%async_computation.19 | async-start | bytes 1310720 | tf_op jit(solution)/shard_map/reduce_scatter | solution.py:272
  1137.7 3.5 copy-start.38
  1141.2 132.3 %reduce-scatter.20.cloned.1.call-start = ((), (), s32[]{:S(2)}) async-start(), calls=%async_computation.21 | async-start | bytes 5242880 | tf_op jit(solution)/shard_map/reduce_scatter | solution.py:278
  1147.8 205.8 %reduce-scatter.14.cloned.1.call-start = ((), (), s32[]{:S(2)}) async-start(), calls=%async_computation.18 | async-start | bytes 5242880 | tf_op jit(solution)/shard_map/reduce_scatter | solution.py:269
  1148.3 3.3 copy-start.17
  1161.0 390.2 %reduce-scatter.26.cloned.1.call-start = ((), (), s32[]{:S(2)}) async-start(), calls=%async_computation.24 | async-start | bytes 14417920 | tf_op jit(solution)/shard_map/reduce_scatter | solution.py:290
  1172.1 577.4 %reduce-scatter.24.cloned.1.call-start = ((), (), s32[]{:S(2)}) async-start(), calls=%async_computation.23 | async-start | bytes 14417920 | tf_op jit(solution)/shard_map/reduce_scatter | solution.py:287
  1182.9 764.8 %reduce-scatter.22.cloned.1.call-start = ((), (), s32[]{:S(2)}) async-start(), calls=%async_computation.22 | async-start | bytes 14417920 | tf_op jit(solution)/shard_map/reduce_scatter | solution.py:284
  1193.9 843.7 %all-reduce.17.cloned.1.call-start = ((), (), s32[]{:S(2)}) async-start(), calls=%async_computation.28 | async-start | bytes 6291456 | tf_op jit(solution)/shard_map/psum | solution.py:149
  1194.0 10.9 copy-start.20
  1194.0 10.9 copy-start.33
  1204.9 1.9 copy-start.21
  1210.0 1033.0 %all-reduce.15.cloned.1.call-start = ((), (), s32[]{:S(2)}) async-start(), calls=%async_computation.27 | async-start | bytes 22544384 | tf_op jit(solution)/shard_map/psum | solution.py:298
  1947.7 92.9 %copy-start.41 = (bf16[2048]{0:T(1024)(128)(2,1)S(1)}, bf16[2048]{0:T(1024)(128)(2,1)}, u32[]{:S(2)}) copy-start(bf16[2048]{0:T(1024)(128)(2,1)} %get-tuple-element.11) | copy-start | bytes 12292
  2060.2 3.1 copy-start.6
  2060.2 3.1 copy-start.11
  2060.2 4.0 copy-start.18
  2242.9 6.6 copy-start.30
  2246.6 4.6 copy-start.25
  2251.1 2.9 copy-start.24
  2254.1 2.9 copy-start.23
  (8 other events, 10.4 us)
Sparse Core Ops, SparseCore 0:
  9.6 30.6 all-gather.9
  41.9 27.3 all-gather.11
  70.9 80.2 all-gather.13
  152.6 79.2 all-gather.15
  237.8 84.2 all-reduce.10
  323.6 201.0 all-gather.19
  526.4 199.2 all-gather.17
  727.3 199.2 all-gather.21
  959.4 83.9 all-reduce.12
  1074.0 23.2 reduce-scatter.29
  1113.2 23.3 reduce-scatter.27
  1139.3 27.1 reduce-scatter.17
  1169.5 25.7 reduce-scatter.15
  1198.0 75.4 reduce-scatter.19
  1276.3 77.2 reduce-scatter.13
  1355.8 195.4 reduce-scatter.25
  1553.5 195.9 reduce-scatter.23
  1751.7 195.9 reduce-scatter.21
  1950.7 86.9 all-reduce.16
  2041.1 201.7 all-reduce.14
where the time goes:
time: 2270 us
  waiting for transfers between devices  1910 us (84%)
  matrix products  189 us (8%)
  blocking collectives  61.3 us (3%)
  other arithmetic  60.2 us (3%)
  local copies, waits for them, and re-layouts  32.7 us (1%)
    reduce_scatter x1, waiting for transfers between devices, body(): lax.psum_scatter(grad_gate.astype(jnp.bfloat16), 'fsdp', scatter_dimensio...  198 us
    reduce_scatter x1, waiting for transfers between devices, body(): lax.psum_scatter(grad_up.astype(jnp.bfloat16), 'fsdp', scatter_dimension=...  198 us
    all_gather x1, waiting for transfers between devices, ffn_weights(): lax.all_gather(w_up, 'fsdp', axis=0, tiled=True)  198 us
    reduce_scatter x1, waiting for transfers between devices, body(): lax.psum_scatter(grad_down.astype(jnp.bfloat16), 'fsdp', scatter_dimensio...  198 us
    all_gather x1, waiting for transfers between devices, ffn_weights(): lax.all_gather(w_gate, 'fsdp', axis=0, tiled=True)  189 us
    all_gather x1, waiting for transfers between devices, ffn_weights(): lax.all_gather(w_down, 'fsdp', axis=1, tiled=True)  189 us
    psum x1, waiting for transfers between devices, body(): lax.psum(shard_query.astype(jnp.bfloat16), 'ctx').astype(jnp.float32)  177 us
    psum x1, waiting for transfers between devices, body(): lax.psum(jnp.dot(hidden_b, full_down, preferred_element_type=jnp.float32)...  88.1 us
  transfers between devices with their start and end apart: 20, of which 17 were waited for; matrix products, arithmetic and copies ran while one was open for 8% of the time, Pallas kernels for 0%

commit v1 on v0

--- a/solution.py
+++ b/solution.py
@@ -7,6 +7,29 @@
 HEAD = 128
 norm_eps = 1e-05
 rope_base = 10000.0
+
+
+def joined_along(blocks, dim):
+    blocks = jnp.moveaxis(blocks, 0, dim)
+    dims = blocks.shape
+    return blocks.reshape(*dims[:dim], dims[dim] * dims[dim + 1], *dims[dim + 2 :])
+
+
+def grow_blocks(shard, axis):
+    size, here = (lax.axis_size(axis), lax.axis_index(axis))
+    blocks, bit = (shard[None], 1)
+    while bit < size:
+        received = lax.ppermute(blocks, axis, [(i, i ^ bit) for i in range(size)])
+        low = here & bit == 0
+        blocks = jnp.concatenate(
+            [jnp.where(low, blocks, received), jnp.where(low, received, blocks)]
+        )
+        bit *= 2
+    return blocks
+
+
+def gather_by_bits(array, axis, dim):
+    return joined_along(grow_blocks(array, axis), dim)
 
 
 def rotate(values_in, positions, sign):
@@ -78,7 +101,7 @@
 
     def attn_weights():
         return (
-            lax.all_gather(w_query, "fsdp", axis=0, tiled=True),
+            gather_by_bits(w_query, "fsdp", 0),
             lax.all_gather(w_key, "fsdp", axis=0, tiled=True),
             lax.all_gather(w_value, "fsdp", axis=0, tiled=True),
             lax.all_gather(w_out, "fsdp", axis=1, tiled=True),

time: 2270 us -> 2310 us (1.018)
  blocking collectives: 61.3 us -> 93.5 us
    ppermute x0 -> x2, waiting for transfers between devices: none -> 84 us  [grow_blocks(): received = lax.ppermute(blocks, axis, [(i, i ^ bit) for i in range(size)])]
    all_gather x1 -> x0, waiting for transfers between devices: 68.4 us -> none  [attn_weights(): lax.all_gather(w_query, 'fsdp', axis=0, tiled=True)]
    all_gather x1, waiting for transfers between devices: 50.7 us -> 0.02 us  [attn_weights(): lax.all_gather(w_out, 'fsdp', axis=1, tiled=True)]
    all_gather x1, waiting for transfers between devices: 17.4 us -> 53.9 us  [attn_weights(): lax.all_gather(w_key, 'fsdp', axis=0, tiled=True)]
    all_gather x1, blocking collectives: 13.7 us -> 45.7 us  [attn_weights(): lax.all_gather(gain_attn, 'fsdp', axis=0, tiled=True)]
  transfers between devices with their start and end apart: 20 -> 21, of which waited for: 17 -> 15; matrix products, arithmetic and copies ran while one was open for 8% -> 9% of each run, Pallas kernels for 0% -> 0%
where the time goes in v1:
time: 2310 us; the launch traced here: 2300 us
  waiting for transfers between devices  1890 us (82%)
  matrix products  189 us (8%)
  blocking collectives  93.5 us (4%)
  other arithmetic  70.4 us (3%)
  local copies, waits for them, and re-layouts  34.9 us (2%)
    reduce_scatter x1, waiting for transfers between devices, body(): lax.psum_scatter(grad_up.astype(jnp.bfloat16), 'fsdp', scatter_dimension=...  198 us
    reduce_scatter x1, waiting for transfers between devices, body(): lax.psum_scatter(grad_gate.astype(jnp.bfloat16), 'fsdp', scatter_dimensio...  198 us
    all_gather x1, waiting for transfers between devices, ffn_weights(): lax.all_gather(w_up, 'fsdp', axis=0, tiled=True)  198 us
    reduce_scatter x1, waiting for transfers between devices, body(): lax.psum_scatter(grad_down.astype(jnp.bfloat16), 'fsdp', scatter_dimensio...  198 us
    all_gather x1, waiting for transfers between devices, ffn_weights(): lax.all_gather(w_down, 'fsdp', axis=1, tiled=True)  189 us
    all_gather x1, waiting for transfers between devices, ffn_weights(): lax.all_gather(w_gate, 'fsdp', axis=0, tiled=True)  189 us
    psum x1, waiting for transfers between devices, body(): lax.psum(shard_query.astype(jnp.bfloat16), 'ctx').astype(jnp.float32)  177 us
    psum x1, waiting for transfers between devices, body(): lax.psum(jnp.dot(hidden_b, full_down, preferred_element_type=jnp.float32)...  87.9 us
  transfers between devices with their start and end apart: 21, of which 15 were waited for; matrix products, arithmetic and copies ran while one was open for 9% of the time, Pallas kernels for 0%

profile of v1, /device:TPU:0, one launch (start us, length us, event | category | flops | bytes accessed | tf_op | source)
XLA Modules:
  0.0 2301.7 jit_solution(16815099684039483531)
XLA Ops:
  8.7 3.1 collective-permute-start
  13.3 45.7 %all-gather = bf16[4,1,512]{2,1,0:T(2,128)(2,1)S(1)} all-gather(bf16[1,1,512]{2,1,0:T(2,128)(2,1)S(1)} %reshape.384), channel_id=1, replica_groups=mesh['fsdp'=4,'ctx'=4,'tp'=2] {'fsdp'}, dimensions={0}, use_global_device_ids=true | all-gather | bytes 5120 | tf_op jit(solution)/shard_map/all_gather | solution.py:108
  70.9 8.6 all_gather.40
  80.7 53.9 %all-gather.11.cloned.1.call-done = bf16[2048,256]{1,0:T(8,128)(2,1)} async-done(((bf16[512,256]{1,0:T(8,128)(2,1)}), bf16[2048,256]{1,0:T(8,128)(2,1)}) %all-gather.11.cloned.1.call-update) | async-done | bytes 1048592 | tf_op jit(solution)/shard_map/all_gather | solution.py:105
  134.6 2.3 copy.103
  136.9 2.2 fusion.73
  139.1 9.0 all_gather.42
  148.2 84.0 %collective-permute-done.1 = bf16[2,512,1024]{2,1,0:T(8,128)(2,1)} collective-permute-done((bf16[2,512,1024]{2,1,0:T(8,128)(2,1)}, bf16[2,512,1024]{2,1,0:T(8,128)(2,1)}, u32[]{:S(2)}, u32[]{:S(2)}) %collective-permute-start.1) | collective-permute-done | bytes 2097184 | tf_op jit(solution)/shard_map/ppermute | solution.py:22
  234.3 2.4 pad_maximum_fusion
  236.7 6.6 copy.105
  243.3 4.6 fusion.71
  251.4 2.4 fusion.69
  255.3 3.3 fusion.12
  260.4 2.7 fusion.79
  263.2 2.9 fusion.80
  266.3 5.9 fusion.102
  274.3 11.9 all-gather.1
  286.2 71.1 %all-reduce.11.cloned.1.call-done = f32[384,2048]{1,0:T(8,128)} async-done(((f32[384,2048]{1,0:T(8,128)}), f32[384,2048]{1,0:T(8,128)}) %all-reduce.11.cloned.1.call-update) | async-done | bytes 3145744 | tf_op jit(solution)/shard_map/psum | solution.py:162
  357.3 3.0 multiply_reduce_fusion.2
  361.8 198.1 %all-gather.17.cloned.1.call-done = bf16[2048,2816]{1,0:T(8,128)(2,1)} async-done(((bf16[512,2816]{1,0:T(8,128)(2,1)}), bf16[2048,2816]{1,0:T(8,128)(2,1)}) %all-gather.17.cloned.1.call-update) | async-done | bytes 11534352 | tf_op jit(solution)/shard_map/all_gather | solution.py:114
  559.9 11.4 fusion.104
  571.3 189.4 %all-gather.15.cloned.1.call-done = bf16[2048,2816]{1,0:T(8,128)(2,1)} async-done(((bf16[512,2816]{1,0:T(8,128)(2,1)}), bf16[2048,2816]{1,0:T(8,128)(2,1)}) %all-gather.15.cloned.1.call-update) | async-done | bytes 11534352 | tf_op jit(solution)/shard_map/all_gather | solution.py:113
  760.7 11.4 fusion.103
  772.1 189.5 %all-gather.19.cloned.1.call-done = bf16[2816,2048]{1,0:T(8,128)(2,1)} async-done(((bf16[2816,512]{1,0:T(8,128)(2,1)}), bf16[2816,2048]{1,0:T(8,128)(2,1)}) %all-gather.19.cloned.1.call-update) | async-done | bytes 11534352 | tf_op jit(solution)/shard_map/all_gather | solution.py:115
  961.6 12.9 multiply_convert_fusion
  974.5 9.1 fusion.105
  983.6 10.6 convolution_add_fusion
  994.3 84.1 %all-reduce.13.cloned.1.call-done = f32[384,2048]{1,0:T(8,128)} async-done(((f32[384,2048]{1,0:T(8,128)}), f32[384,2048]{1,0:T(8,128)}) %all-reduce.13.cloned.1.call-update) | async-done | bytes 3145744 | tf_op jit(solution)/shard_map/psum | solution.py:191
  1078.4 3.4 multiply_reduce_fusion
  1084.8 2.7 convolution_convert_fusion.8
  1087.5 2.8 reshape.376
  1091.8 6.1 fusion.87
  1097.9 5.7 fusion.62
  1106.6 2.3 copy.150
  1109.0 16.4 fusion.3
  1125.4 13.9 fusion.5
  1145.7 2.3 copy.148
  1148.2 3.3 convolution_convert_fusion.6
  1151.6 20.1 reduce-scatter.28.cloned.1.call-done
  1172.9 3.3 convolution_convert_fusion.7
  1176.2 6.5 convolution_convert_fusion.3
  1183.3 3.3 convolution_bitcast_fusion.3
  1186.6 3.2 convolution_bitcast_fusion.2
  1191.5 4.5 convolution_convert_fusion.4
  1196.1 11.0 convolution_convert_fusion.2
  1207.2 10.7 convolution_convert_fusion
  1218.1 10.8 convolution_convert_fusion.1
  1229.0 10.8 convolution_convert_fusion.5
  1243.3 3.0 add_convert_fusion
  1246.4 61.7 %reduce-scatter.20.cloned.1.call-done = bf16[1024,512]{1,0:T(8,128)(2,1)} async-done(((bf16[1024,2048]{1,0:T(8,128)(2,1)}), bf16[1024,512]{1,0:T(8,128)(2,1)}) %reduce-scatter.20.cloned.1.call-update) | async-done | bytes 1048592 | tf_op jit(solution)/shard_map/reduce_scatter | solution.py:301
  1308.1 80.1 %reduce-scatter.14.cloned.1.call-done = bf16[512,1024]{1,0:T(8,128)(2,1)} async-done(((bf16[2048,1024]{1,0:T(8,128)(2,1)}), bf16[512,1024]{1,0:T(8,128)(2,1)}) %reduce-scatter.14.cloned.1.call-update) | async-done | bytes 1048592 | tf_op jit(solution)/shard_map/reduce_scatter | solution.py:292
  1388.2 197.7 %reduce-scatter.26.cloned.1.call-done = bf16[2816,512]{1,0:T(8,128)(2,1)} async-done(((bf16[2816,2048]{1,0:T(8,128)(2,1)}), bf16[2816,512]{1,0:T(8,128)(2,1)}) %reduce-scatter.26.cloned.1.call-update) | async-done | bytes 2883600 | tf_op jit(solution)/shard_map/reduce_scatter | solution.py:313
  1585.9 198.2 %reduce-scatter.24.cloned.1.call-done = bf16[512,2816]{1,0:T(8,128)(2,1)} async-done(((bf16[2048,2816]{1,0:T(8,128)(2,1)}), bf16[512,2816]{1,0:T(8,128)(2,1)}) %reduce-scatter.24.cloned.1.call-update) | async-done | bytes 2883600 | tf_op jit(solution)/shard_map/reduce_scatter | solution.py:310
  1784.1 198.2 %reduce-scatter.22.cloned.1.call-done = bf16[512,2816]{1,0:T(8,128)(2,1)} async-done(((bf16[2048,2816]{1,0:T(8,128)(2,1)}), bf16[512,2816]{1,0:T(8,128)(2,1)}) %reduce-scatter.22.cloned.1.call-update) | async-done | bytes 2883600 | tf_op jit(solution)/shard_map/reduce_scatter | solution.py:307
  1984.2 87.9 %all-reduce.17.cloned.1.call-done = (bf16[384,2048]{1,0:T(8,128)(2,1)}, bf16[384,2048]{1,0:T(8,128)(2,1)}) async-done(((bf16[384,2048]{1,0:T(8,128)(2,1)}, bf16[384,2048]{1,0:T(8,128)(2,1)}), (bf16[384,2048]{1,0:T(8,128)(2,1)}, bf16[384,2048]{1,0:T(8,128)(2,1)})) %all-reduce.17.cloned.1.call-update) | async-done | bytes 3145744 | tf_op jit(solution)/shard_map/psum | solution.py:172
  2072.1 3.0 fusion.38
  2075.1 11.9 all-reduce.4
  2087.1 6.4 all-reduce.2
  2094.7 3.1 fusion.67
  2100.8 176.7 %all-reduce.15.cloned.1.call-done = (bf16[512,1024]{1,0:T(8,128)(2,1)}, bf16[512,256]{1,0:T(8,128)(2,1)}, bf16[512,256]{1,0:T(8,128)(2,1)}, bf16[1024,512]{1,0:T...) async-done(((bf16[512,1024]{1,0:T(8,128)(2,1)}, bf16[512,256]{1,0:T(8,128)(2,1)}, bf16[512,256]{1,0:T(8,128)(2,1)}, ...) | async-done | bytes 11272208 | tf_op jit(solution)/shard_map/psum | solution.py:321
  2281.1 2.9 convert_element_type.285
  2285.7 2.9 convert_element_type.293
  2288.7 2.9 convert_element_type.295
  2291.6 3.4 convert_element_type.297
  (217 shorter events, 60.6 us)
Async XLA Ops:
  7.2 57.0 %copy-start.33 = (bf16[512,1024]{1,0:T(8,128)(2,1)S(1)}, bf16[512,1024]{1,0:T(8,128)(2,1)}, u32[]{:S(2)}) copy-start(bf16[512,1024]{1,0:T(8,128)(2,1)} %param.20) | copy-start | bytes 3145732
  7.2 61.7 %all-gather.9.cloned.1.call-start = ((), (), s32[]{:S(2)}) async-start(), calls=%async_computation.9 | async-start | bytes 1310720 | tf_op jit(solution)/shard_map/all_gather | solution.py:106
  7.9 126.7 %all-gather.11.cloned.1.call-start = ((), (), s32[]{:S(2)}) async-start(), calls=%async_computation.10 | async-start | bytes 1310720 | tf_op jit(solution)/shard_map/all_gather | solution.py:105
  8.7 257.6 %all-gather.13.cloned.1.call-start = ((), (), s32[]{:S(2)}) async-start(), calls=%async_computation.11 | async-start | bytes 5242880 | tf_op jit(solution)/shard_map/all_gather | solution.py:107
  8.7 55.5 %collective-permute-start = (bf16[1,512,1024]{2,1,0:T(8,128)(2,1)}, bf16[1,512,1024]{2,1,0:T(8,128)(2,1)}, u32[]{:S(2)}, u32[]{:S(2)}) collective-permute-start(bf16[1,512,1024]{2,1,0:T(8,128)(2,1)} %bitcast.332), channel_id=1, source_target_pairs={{0,8},{8,0},{16,24},{24,16},{1,9},{9,1},{17,25},{25,17},{2,10},{10... | collective-permute-start | bytes 3145736 | tf_op jit(solution)/shard_map/ppermute | solution.py:22
  11.8 345.5 %all-reduce.11.cloned.1.call-start = ((), (), s32[]{:S(2)}) async-start(), calls=%async_computation.12 | async-start | bytes 6291456 | tf_op jit(solution)/shard_map/psum | solution.py:162
  59.0 184.3 %copy-start.40 = (f32[4,1,512]{2,1,0:T(1,128)}, f32[4,1,512]{2,1,0:T(1,128)S(1)}, u32[]{:S(2)}) copy-start(f32[4,1,512]{2,1,0:T(1,128)S(1)} %convert_element_type.304) | copy-start | bytes 24580
  63.1 180.2 %copy-start.44 = (f32[384]{0:T(512)}, f32[384]{0:T(512)S(1)}, u32[]{:S(2)}) copy-start(f32[384]{0:T(512)S(1)} %add_rsqrt_fusion.1) | copy-start | bytes 4612
  64.2 183.7 %copy-start.30 = (f32[384,64]{0,1:T(8,128)}, f32[384,64]{0,1:T(8,128)S(1)}, u32[]{:S(2)}) copy-start(f32[384,64]{0,1:T(8,128)S(1)} %get-tuple-element.57) | copy-start | bytes 294916
  65.6 3.2 copy-start.4
  67.2 165.0 %collective-permute-start.1 = (bf16[2,512,1024]{2,1,0:T(8,128)(2,1)}, bf16[2,512,1024]{2,1,0:T(8,128)(2,1)}, u32[]{:S(2)}, u32[]{:S(2)}) collective-permute-start(bf16[2,512,1024]{2,1,0:T(8,128)(2,1)} %pad_maximum_fusion.1), channel_id=1, source_target_pairs={{0,16},{8,24},{16,0},{24,8},{1,17},{9,25},{17,1},{25,9},{2,18},{10... | collective-permute-start | bytes 6291464 | tf_op jit(solution)/shard_map/ppermute | solution.py:22
  68.8 194.4 %copy-start.7 = (pred[384,1536]{0,1:T(8,128)(4,1)}, pred[384,1536]{0,1:T(8,128)(4,1)S(1)}, u32[]{:S(2)}) copy-start(pred[384,1536]{0,1:T(8,128)(4,1)S(1)} %fusion.58) | copy-start | bytes 1769476
  136.9 95.3 %copy-start.15 = (bf16[1,512,1024]{2,1,0:T(8,128)(2,1)S(1)}, bf16[1,512,1024]{2,1,0:T(8,128)(2,1)}, u32[]{:S(2)}) copy-start(bf16[1,512,1024]{2,1,0:T(8,128)(2,1)} %copy-done.14) | copy-start | bytes 3145732
  136.9 95.3 %copy-start.17 = (bf16[1,512,1024]{2,1,0:T(8,128)(2,1)S(1)}, bf16[1,512,1024]{2,1,0:T(8,128)(2,1)}, u32[]{:S(2)}) copy-start(bf16[1,512,1024]{2,1,0:T(8,128)(2,1)} %copy-done.16) | copy-start | bytes 3145732
  249.8 4.0 copy-start.21
  255.3 5.1 copy-start
  258.7 4.5 copy-start.1
  266.3 6.0 copy-start.24
  272.3 287.6 %all-gather.17.cloned.1.call-start = ((), (), s32[]{:S(2)}) async-start(), calls=%async_computation.14 | async-start | bytes 14417920 | tf_op jit(solution)/shard_map/all_gather | solution.py:114
  272.9 13.3 copy-start.47
  272.9 487.8 %all-gather.15.cloned.1.call-start = ((), (), s32[]{:S(2)}) async-start(), calls=%async_computation.13 | async-start | bytes 14417920 | tf_op jit(solution)/shard_map/all_gather | solution.py:113
  273.5 688.2 %all-gather.19.cloned.1.call-start = ((), (), s32[]{:S(2)}) async-start(), calls=%async_computation.15 | async-start | bytes 14417920 | tf_op jit(solution)/shard_map/all_gather | solution.py:115
  274.2 804.2 %all-reduce.13.cloned.1.call-start = ((), (), s32[]{:S(2)}) async-start(), calls=%async_computation.16 | async-start | bytes 6291456 | tf_op jit(solution)/shard_map/psum | solution.py:191
  286.2 796.5 %copy-start.42 = (f32[384]{0:T(512)}, f32[384]{0:T(512)S(1)}, u32[]{:S(2)}) copy-start(f32[384]{0:T(512)S(1)} %convert_reduce_fusion) | copy-start | bytes 4612
  974.5 9.1 copy-start.50
  974.5 9.1 copy-start.51
  994.3 153.9 %reduce-scatter.30.cloned.1.call-start = ((), (), s32[]{:S(2)}) async-start(), calls=%async_computation.25 | async-start | bytes 983040
  1078.4 3.4 copy-start.13
  1078.4 3.4 copy-start.32
  1081.8 3.0 copy-start.18
  1091.7 6.1 copy-start.8
  1091.7 11.9 slice-start
  1091.7 11.9 slice-start.1
  1097.9 5.8 slice-start.2
  1108.9 62.7 %reduce-scatter.28.cloned.1.call-start = ((), (), s32[]{:S(2)}) async-start(), calls=%async_computation.24 | async-start | bytes 983040
  1109.0 16.4 copy-start.9
  1125.4 14.0 copy-start.20
  1139.4 3.7 copy-start.2
  1144.8 3.4 copy-start.41
  1144.8 3.4 copy-start.45
  1148.1 24.7 %copy-start.31 = (f32[384,64]{0,1:T(8,128)S(1)}, f32[384,64]{0,1:T(8,128)}, u32[]{:S(2)}) copy-start(f32[384,64]{0,1:T(8,128)} %copy-done.30) | copy-start | bytes 294916
  1148.1 24.7 %copy-start.36 = (f32[384,64]{0,1:T(8,128)S(1)}, f32[384,64]{0,1:T(8,128)}, u32[]{:S(2)}) copy-start(f32[384,64]{0,1:T(8,128)} %get-tuple-element.55) | copy-start | bytes 294916
  1148.1 98.3 %reduce-scatter.18.cloned.1.call-start = ((), (), s32[]{:S(2)}) async-start(), calls=%async_computation.19 | async-start | bytes 1310720 | tf_op jit(solution)/shard_map/reduce_scatter | solution.py:298
  1151.5 94.9 %reduce-scatter.16.cloned.1.call-start = ((), (), s32[]{:S(2)}) async-start(), calls=%async_computation.18 | async-start | bytes 1310720 | tf_op jit(solution)/shard_map/reduce_scatter | solution.py:295
  1172.7 3.5 copy-start.43
  1176.2 131.9 %reduce-scatter.20.cloned.1.call-start = ((), (), s32[]{:S(2)}) async-start(), calls=%async_computation.20 | async-start | bytes 5242880 | tf_op jit(solution)/shard_map/reduce_scatter | solution.py:301
  1182.8 205.4 %reduce-scatter.14.cloned.1.call-start = ((), (), s32[]{:S(2)}) async-start(), calls=%async_computation.17 | async-start | bytes 5242880 | tf_op jit(solution)/shard_map/reduce_scatter | solution.py:292
  1183.3 3.3 copy-start.22
  1196.0 389.8 %reduce-scatter.26.cloned.1.call-start = ((), (), s32[]{:S(2)}) async-start(), calls=%async_computation.23 | async-start | bytes 14417920 | tf_op jit(solution)/shard_map/reduce_scatter | solution.py:313
  1207.1 577.0 %reduce-scatter.24.cloned.1.call-start = ((), (), s32[]{:S(2)}) async-start(), calls=%async_computation.22 | async-start | bytes 14417920 | tf_op jit(solution)/shard_map/reduce_scatter | solution.py:310
  1217.9 764.4 %reduce-scatter.22.cloned.1.call-start = ((), (), s32[]{:S(2)}) async-start(), calls=%async_computation.21 | async-start | bytes 14417920 | tf_op jit(solution)/shard_map/reduce_scatter | solution.py:307
  1228.9 10.9 copy-start.39
  1229.0 843.2 %all-reduce.17.cloned.1.call-start = ((), (), s32[]{:S(2)}) async-start(), calls=%async_computation.27 | async-start | bytes 6291456 | tf_op jit(solution)/shard_map/psum | solution.py:172
  1229.0 10.8 copy-start.35
  1241.1 2.2 copy-start.10
  1246.3 1031.2 %all-reduce.15.cloned.1.call-start = ((), (), s32[]{:S(2)}) async-start(), calls=%async_computation.26 | async-start | bytes 22544384 | tf_op jit(solution)/shard_map/psum | solution.py:321
  1982.3 92.8 %copy-start.46 = (bf16[2048]{0:T(1024)(128)(2,1)S(1)}, bf16[2048]{0:T(1024)(128)(2,1)}, u32[]{:S(2)}) copy-start(bf16[2048]{0:T(1024)(128)(2,1)} %get-tuple-element.11) | copy-start | bytes 12292
  2094.7 3.1 copy-start.6
  2094.7 3.1 copy-start.12
  2094.7 4.0 copy-start.23
  2277.5 6.6 copy-start.34
  2281.1 4.6 copy-start.29
  2285.7 2.9 copy-start.28
  2288.7 2.9 copy-start.27
  (12 other events, 18.5 us)
Sparse Core Ops, SparseCore 0:
  9.6 41.8 all-gather.8
  53.0 81.5 all-gather.10
  136.2 104.5 all-gather.12
  272.4 84.8 all-reduce.10
  358.8 201.0 all-gather.16
  561.4 199.2 all-gather.14
  762.3 199.2 all-gather.18
  994.4 83.9 all-reduce.12
  1109.0 23.2 reduce-scatter.29
  1148.2 23.3 reduce-scatter.27
  1174.5 27.1 reduce-scatter.17
  1204.5 25.7 reduce-scatter.15
  1232.6 75.4 reduce-scatter.19
  1310.9 77.2 reduce-scatter.13
  1390.4 195.4 reduce-scatter.25
  1588.1 195.9 reduce-scatter.23
  1786.3 195.9 reduce-scatter.21
  1985.1 86.9 all-reduce.16
  2075.7 201.7 all-reduce.14
